TPU v7x, 32 devices: a whole 2x2x4 slice. The times are simulated.
32 devices in a mesh: dp: 8 (over z, y), seq: 4 (over x, core).
Axes of the slice: x: 2, y: 2, z: 4, core: 2. Of those that a mesh axis runs over, the one named last changes fastest.
Arguments:
- hidden_in: bfloat16 [32, 1024, 768], P('dp', 'seq'), may hold values from -6 to 6
- time_table: bfloat16 [1024, 128], replicated, may hold values from -6 to 6
- time_step: int32 [32], P('dp'), may hold values from 0 to 1023
- token_pos: int32 [32, 1024], P('dp', 'seq'), may hold values from 0 to 3071, as said below
- heads_weight: bfloat16 [768, 2304], P('seq'), may hold values from -0.15625 to 0.15625
- merge_weight: bfloat16 [768, 768], P('seq'), may hold values from -1.75 to 1.75
- lift_weight: bfloat16 [768, 3072], P('seq'), may hold values from -0.21875 to 0.21875
- lift_bias: bfloat16 [3072], P('seq'), may hold values from -3 to 3
- drop_weight: bfloat16 [3072, 768], P('seq'), may hold values from -0.109375 to 0.109375
- drop_bias: bfloat16 [768], P('seq'), may hold values from -3 to 3
- modulate_weight: bfloat16 [4608, 128], P('seq'), may hold values from -0.5 to 0.5
- modulate_bias: bfloat16 [4608], P('seq'), may hold values from -3 to 3
- first_gain: bfloat16 [768], P('seq'), may hold values from 0.099609375 to 1.8984375
- second_gain: bfloat16 [768], P('seq'), may hold values from 0.099609375 to 1.8984375
- out_grad: bfloat16 [32, 1024, 768], P('dp', 'seq'), may hold values from -6 to 6
Outputs:
- block_out: bfloat16 [32, 1024, 768], P('dp', 'seq')
- input_grad: bfloat16 [32, 1024, 768], P('dp', 'seq')
- heads_grad: float32 [768, 2304], P('seq')
- merge_grad: float32 [768, 768], P('seq')
- lift_grad: float32 [768, 3072], P('seq')
- liftbias_grad: float32 [3072], P('seq')
- drop_grad: float32 [3072, 768], P('seq')
- dropbias_grad: float32 [768], P('seq')
- modulate_grad: float32 [4608, 128], P('seq')
- modulatebias_grad: float32 [4608], P('seq')
- firstgain_grad: float32 [768], P('seq')
- secondgain_grad: float32 [768], P('seq')
- table_grad: float32 [1024, 128], P('seq')
Inputs may be any that keep to these rules, and one draw needn't show every extreme that they name: `token_pos`: positions count up by one along a row and start again at 0 at each separator token; in every aligned group of 4 rows one row holds no separator; such a row in the first group starts at 2048, such a row in the second group starts at 0.
All inputs are finite; a program needn't handle non-finite values.
Results may differ from a plain program's by a relative error of at most 0.017.
The roundings to bfloat16 on the way count: a program that leaves them out, or rounds other values in their place, can miss the bound.
Values may be sent and summed in bfloat16 or wider, within the bound.
No kernel may reach another device: no remote copies, remote signals or barrier semaphores. Data moves between devices by JAX's collectives and lax.ppermute only.
A program may use at most 320 MiB of HBM per device.

v0:
```python
from functools import partial
import math
import jax
import jax.numpy as jnp
from jax import lax
from jax.sharding import PartitionSpec as P

HEADS = 12
EPSILON = 1e-05


def rotate_half(values):
    middle = values.shape[-1] // 2
    return jnp.concatenate([-values[..., middle:], values[..., :middle]], axis=-1)


def rotate(values, cosine, sine):
    return values * cosine + rotate_half(values) * sine


def unrotate(values, cosine, sine):
    return values * cosine - rotate_half(values * sine)


def norm_forward(values, gain):
    center = values - jnp.mean(values, axis=-1, keepdims=True)
    inverse = lax.rsqrt(jnp.mean(center * center, axis=-1, keepdims=True) + EPSILON)
    unit = center * inverse
    return (unit, inverse, unit * gain)


def norm_backward(normed_grad, unit, inverse, gain):
    unit_grad = normed_grad * gain
    first = jnp.mean(unit_grad, axis=-1, keepdims=True)
    second = jnp.mean(unit_grad * unit, axis=-1, keepdims=True)
    return inverse * (unit_grad - first - unit * second)


def grouping(seqs, span):
    group = 1
    while group * span < 512 and seqs % (group * 2) == 0:
        group = group * 2
    return group


def shards(
    hidden_in,
    time_table,
    time_step,
    token_pos,
    heads_weight,
    merge_weight,
    lift_weight,
    lift_bias,
    drop_weight,
    drop_bias,
    modulate_weight,
    modulate_bias,
    first_gain,
    second_gain,
    out_grad,
):
    float_type = jnp.float32
    low_type = jnp.bfloat16
    position_count = lax.axis_size("seq")
    hidden_rows, upstream_rows, places_rows = (hidden_in, out_grad, token_pos)
    seqs, span, width = hidden_rows.shape
    length = span * position_count
    head_width = width // HEADS
    scale = 1.0 / math.sqrt(head_width)
    gathered = (
        lax.all_gather(heads_weight, "seq", axis=0, tiled=True),
        lax.all_gather(merge_weight, "seq", axis=0, tiled=True),
        lax.all_gather(lift_weight, "seq", axis=0, tiled=True),
        lax.all_gather(lift_bias, "seq", axis=0, tiled=True),
        lax.all_gather(drop_weight, "seq", axis=0, tiled=True),
        lax.all_gather(drop_bias, "seq", axis=0, tiled=True),
        lax.all_gather(modulate_weight, "seq", axis=0, tiled=True),
        lax.all_gather(modulate_bias, "seq", axis=0, tiled=True),
        lax.all_gather(first_gain, "seq", axis=0, tiled=True),
        lax.all_gather(second_gain, "seq", axis=0, tiled=True),
    )
    w_heads, w_merge, w_lift, b_lift, w_drop, b_drop, w_mod, b_mod, gain_one, gain_two = gathered
    gain_one = gain_one.astype(float_type)
    gain_two = gain_two.astype(float_type)
    table_rows = time_table.shape[0]
    choose = (time_step[:, None] == jnp.arange(table_rows, dtype=jnp.int32)[None, :]).astype(
        low_type
    )
    conds = jnp.dot(choose, time_table, preferred_element_type=float_type)
    modulation = lax.dot_general(
        conds.astype(low_type), w_mod, (((1,), (1,)), ((), ())), preferred_element_type=float_type
    ) + b_mod.astype(float_type)
    pieces = [piece[:, None, :] for piece in jnp.split(modulation, 6, axis=-1)]
    shift_a, scale_a, gate_a, shift_b, scale_b, gate_b = pieces
    positions = places_rows.astype(float_type)
    freqs = 10000.0 ** (-jnp.arange(0, head_width, 2, dtype=float_type) / head_width)
    angles = positions[..., None] * freqs
    angles = jnp.concatenate([angles, angles], axis=-1)
    cosine = jnp.cos(angles)[:, :, None, :]
    sine = jnp.sin(angles)[:, :, None, :]
    head_layout = (seqs, span, HEADS, head_width)
    inputs = hidden_rows.astype(float_type)
    unit_one, inverse_one, normed_one = norm_forward(inputs, gain_one)
    adapted_one = (normed_one * (1.0 + scale_a) + shift_a).astype(low_type)
    projected = jnp.einsum("scd,de->sce", adapted_one, w_heads, preferred_element_type=float_type)
    query_raw, key_raw, value_raw = jnp.split(projected, 3, axis=-1)
    query = rotate(query_raw.reshape(head_layout), cosine, sine).astype(low_type)
    keys_local = (
        rotate(key_raw.reshape(head_layout), cosine, sine)
        .astype(low_type)
        .reshape(seqs, span, width)
    )
    values_local = value_raw.astype(low_type)
    keys_all, values_all = (
        lax.all_gather(keys_local, "seq", axis=1, tiled=True),
        lax.all_gather(values_local, "seq", axis=1, tiled=True),
    )
    group = grouping(seqs, span)
    blocks = seqs // group

    def split_groups(array):
        return array.reshape((blocks, group) + array.shape[1:])

    def attend(block):
        query_b, keys_b, values_b = block
        keys_h = keys_b.reshape(group, length, HEADS, head_width)
        values_h = values_b.reshape(group, length, HEADS, head_width)
        scores = (
            jnp.einsum("gqhd,gkhd->ghqk", query_b, keys_h, preferred_element_type=float_type)
            * scale
        )
        peak = jnp.max(scores, axis=-1, keepdims=True)
        expos = jnp.exp(scores - peak)
        totals = jnp.sum(expos, axis=-1, keepdims=True)
        probs = (expos / totals).astype(low_type)
        mixed_b = jnp.einsum("ghqk,gkhd->gqhd", probs, values_h, preferred_element_type=float_type)
        return (mixed_b, peak[..., 0] + jnp.log(totals[..., 0]))

    mixed, logsum = lax.map(
        attend, (split_groups(query), split_groups(keys_all), split_groups(values_all))
    )
    mixed_low = mixed.reshape(seqs, span, width).astype(low_type)
    branch = jnp.einsum("scd,de->sce", mixed_low, w_merge, preferred_element_type=float_type)
    middle = inputs + gate_a * branch
    unit_two, inverse_two, normed_two = norm_forward(middle, gain_two)
    adapted_two = (normed_two * (1.0 + scale_b) + shift_b).astype(low_type)
    upper = jnp.einsum(
        "scd,df->scf", adapted_two, w_lift, preferred_element_type=float_type
    ) + b_lift.astype(float_type)
    active, gelu_back = jax.vjp(partial(jax.nn.gelu, approximate=True), upper)
    active_low = active.astype(low_type)
    lowered = jnp.einsum(
        "scf,fd->scd", active_low, w_drop, preferred_element_type=float_type
    ) + b_drop.astype(float_type)
    block_out = (middle + gate_b * lowered).astype(low_type)
    upstream = upstream_rows.astype(float_type)
    gate_b_grad = jnp.sum(upstream * lowered, axis=1)
    lowered_grad = (gate_b * upstream).astype(low_type)
    drop_grad = jnp.einsum(
        "scf,scd->fd", active_low, lowered_grad, preferred_element_type=float_type
    )
    dropbias_grad = jnp.sum(lowered_grad.astype(float_type), axis=(0, 1))
    active_grad = jnp.einsum("scd,fd->scf", lowered_grad, w_drop, preferred_element_type=float_type)
    (upper_grad,) = gelu_back(active_grad)
    upper_low = upper_grad.astype(low_type)
    lift_grad = jnp.einsum("scd,scf->df", adapted_two, upper_low, preferred_element_type=float_type)
    liftbias_grad = jnp.sum(upper_low.astype(float_type), axis=(0, 1))
    adapted_two_grad = jnp.einsum(
        "scf,df->scd", upper_low, w_lift, preferred_element_type=float_type
    )
    shift_b_grad = jnp.sum(adapted_two_grad, axis=1)
    scale_b_grad = jnp.sum(adapted_two_grad * normed_two, axis=1)
    normed_two_grad = adapted_two_grad * (1.0 + scale_b)
    secondgain_grad = jnp.sum(normed_two_grad * unit_two, axis=(0, 1))
    middle_grad = upstream + norm_backward(normed_two_grad, unit_two, inverse_two, gain_two)
    gate_a_grad = jnp.sum(middle_grad * branch, axis=1)
    branch_grad = (gate_a * middle_grad).astype(low_type)
    merge_grad = jnp.einsum(
        "scd,sce->de", mixed_low, branch_grad, preferred_element_type=float_type
    )
    mixed_grad = jnp.einsum(
        "sce,de->scd", branch_grad, w_merge, preferred_element_type=float_type
    ).astype(low_type)
    keys_back, values_back = (
        lax.all_gather(keys_local, "seq", axis=1, tiled=True),
        lax.all_gather(values_local, "seq", axis=1, tiled=True),
    )

    def attend_back(block):
        query_b, keys_b, values_b, logsum_b, mixed_grad_b = block
        keys_h = keys_b.reshape(group, length, HEADS, head_width)
        values_h = values_b.reshape(group, length, HEADS, head_width)
        scores = (
            jnp.einsum("gqhd,gkhd->ghqk", query_b, keys_h, preferred_element_type=float_type)
            * scale
        )
        probs = jnp.exp(scores - logsum_b[..., None])
        probs_low = probs.astype(low_type)
        values_term = jnp.einsum(
            "ghqk,gqhd->gkhd", probs_low, mixed_grad_b, preferred_element_type=float_type
        )
        probs_grad = jnp.einsum(
            "gqhd,gkhd->ghqk", mixed_grad_b, values_h, preferred_element_type=float_type
        )
        center = jnp.sum(probs * probs_grad, axis=-1, keepdims=True)
        scores_grad = (probs * (probs_grad - center)).astype(low_type)
        query_term = (
            jnp.einsum("ghqk,gkhd->gqhd", scores_grad, keys_h, preferred_element_type=float_type)
            * scale
        )
        keys_term = (
            jnp.einsum("ghqk,gqhd->gkhd", scores_grad, query_b, preferred_element_type=float_type)
            * scale
        )
        return (
            query_term,
            keys_term.reshape(group, length, width),
            values_term.reshape(group, length, width),
        )

    mixed_grad_h = mixed_grad.reshape(head_layout)
    query_term, keys_term, values_term = lax.map(
        attend_back,
        (
            split_groups(query),
            split_groups(keys_back),
            split_groups(values_back),
            logsum,
            split_groups(mixed_grad_h),
        ),
    )
    keys_grad, values_grad = (
        lax.psum_scatter(
            keys_term.reshape(seqs, length, width).astype(jnp.bfloat16),
            "seq",
            scatter_dimension=1,
            tiled=True,
        ).astype(jnp.float32),
        lax.psum_scatter(
            values_term.reshape(seqs, length, width).astype(jnp.bfloat16),
            "seq",
            scatter_dimension=1,
            tiled=True,
        ).astype(jnp.float32),
    )
    query_grad = unrotate(query_term.reshape(head_layout), cosine, sine).reshape(seqs, span, width)
    key_grad = unrotate(keys_grad.reshape(head_layout), cosine, sine).reshape(seqs, span, width)
    projected_grad = jnp.concatenate([query_grad, key_grad, values_grad], axis=-1).astype(low_type)
    heads_grad = jnp.einsum(
        "scd,sce->de", adapted_one, projected_grad, preferred_element_type=float_type
    )
    adapted_one_grad = jnp.einsum(
        "sce,de->scd", projected_grad, w_heads, preferred_element_type=float_type
    )
    shift_a_grad = jnp.sum(adapted_one_grad, axis=1)
    scale_a_grad = jnp.sum(adapted_one_grad * normed_one, axis=1)
    normed_one_grad = adapted_one_grad * (1.0 + scale_a)
    firstgain_grad = jnp.sum(normed_one_grad * unit_one, axis=(0, 1))
    input_grad = (
        middle_grad + norm_backward(normed_one_grad, unit_one, inverse_one, gain_one)
    ).astype(low_type)
    modulation_grad = jnp.concatenate(
        [shift_a_grad, scale_a_grad, gate_a_grad, shift_b_grad, scale_b_grad, gate_b_grad], axis=-1
    )
    modulate_grad = jnp.einsum("sm,sc->mc", modulation_grad, conds, precision=lax.Precision.HIGHEST)
    modulatebias_grad = jnp.sum(modulation_grad, axis=0)
    conds_grad = jnp.einsum(
        "sm,mc->sc", modulation_grad, w_mod.astype(float_type), precision=lax.Precision.HIGHEST
    )
    table_grad = jnp.einsum(
        "sn,sc->nc", choose.astype(float_type), conds_grad, precision=lax.Precision.HIGHEST
    )
    terms = (
        heads_grad,
        merge_grad,
        lift_grad,
        liftbias_grad,
        drop_grad,
        dropbias_grad,
        modulate_grad,
        modulatebias_grad,
        firstgain_grad,
        secondgain_grad,
        table_grad,
    )
    shares = (
        lax.psum_scatter(
            terms[0].astype(jnp.bfloat16), "seq", scatter_dimension=0, tiled=True
        ).astype(jnp.float32),
        lax.psum_scatter(
            terms[1].astype(jnp.bfloat16), "seq", scatter_dimension=0, tiled=True
        ).astype(jnp.float32),
        lax.psum_scatter(
            terms[2].astype(jnp.bfloat16), "seq", scatter_dimension=0, tiled=True
        ).astype(jnp.float32),
        lax.psum_scatter(
            terms[3].astype(jnp.bfloat16), "seq", scatter_dimension=0, tiled=True
        ).astype(jnp.float32),
        lax.psum_scatter(
            terms[4].astype(jnp.bfloat16), "seq", scatter_dimension=0, tiled=True
        ).astype(jnp.float32),
        lax.psum_scatter(
            terms[5].astype(jnp.bfloat16), "seq", scatter_dimension=0, tiled=True
        ).astype(jnp.float32),
        lax.psum_scatter(
            terms[6].astype(jnp.bfloat16), "seq", scatter_dimension=0, tiled=True
        ).astype(jnp.float32),
        lax.psum_scatter(
            terms[7].astype(jnp.bfloat16), "seq", scatter_dimension=0, tiled=True
        ).astype(jnp.float32),
        lax.psum_scatter(
            terms[8].astype(jnp.bfloat16), "seq", scatter_dimension=0, tiled=True
        ).astype(jnp.float32),
        lax.psum_scatter(
            terms[9].astype(jnp.bfloat16), "seq", scatter_dimension=0, tiled=True
        ).astype(jnp.float32),
        lax.psum_scatter(
            terms[10].astype(jnp.bfloat16), "seq", scatter_dimension=0, tiled=True
        ).astype(jnp.float32),
    )
    summed = lax.psum(
        (
            shares[0],
            shares[1],
            shares[2],
            shares[3],
            shares[4],
            shares[5],
            shares[6],
            shares[7],
            shares[8],
            shares[9],
            shares[10],
        ),
        "dp",
    )
    return (
        block_out,
        input_grad,
        summed[0],
        summed[1],
        summed[2],
        summed[3],
        summed[4],
        summed[5],
        summed[6],
        summed[7],
        summed[8],
        summed[9],
        summed[10],
    )


def solution(mesh):
    return jax.shard_map(
        shards,
        mesh=mesh,
        in_specs=(
            P("dp", "seq", None),
            P(),
            P("dp"),
            P("dp", "seq"),
            P("seq", None),
            P("seq", None),
            P("seq", None),
            P("seq"),
            P("seq", None),
            P("seq"),
            P("seq", None),
            P("seq"),
            P("seq"),
            P("seq"),
            P("dp", "seq", None),
        ),
        out_specs=(
            P("dp", "seq", None),
            P("dp", "seq", None),
            P("seq", None),
            P("seq", None),
            P("seq", None),
            P("seq"),
            P("seq", None),
            P("seq"),
            P("seq", None),
            P("seq"),
            P("seq"),
            P("seq"),
            P("seq", None),
        ),
        check_vma=False,
    )
```

profile of v0, /device:TPU:0, one launch (start us, length us, event | category | flops | bytes accessed | tf_op | source)
XLA Modules:
  0.0 1162.3 jit_solution(14610913163980127939)
XLA Ops:
  13.3 8.5 all-reduce.10
  22.4 5.2 all-gather
  33.2 29.1 %all-gather.12.cloned.1.call-done = bf16[768,2304]{1,0:T(8,128)(2,1)} async-done(((bf16[192,2304]{1,0:T(8,128)(2,1)}), bf16[768,2304]{1,0:T(8,128)(2,1)}) %all-gather.12.cloned.1.call-update) | async-done | bytes 3538960 | tf_op jit(solution)/shard_map/all_gather | solution.py:72
  62.3 6.2 fusion.52
  68.5 3.6 copy-done.13
  79.2 5.5 split.42
  84.7 3.6 copy.91
  92.5 3.5 copy.92
  96.0 6.6 add_convert_fusion.2
  107.2 5.6 all-gather.1
  121.9 8.7 copy.93
  130.6 37.9 %all-gather.16.cloned.1.call-done = bf16[4,1024,768]{2,1,0:T(8,128)(2,1)} async-done(((bf16[4,256,768]{2,1,0:T(8,128)(2,1)}), bf16[4,1024,768]{2,1,0:T(8,128)(2,1)}) %all-gather.16.cloned.1.call-update) | async-done | bytes 6291472 | tf_op jit(solution)/shard_map/all_gather | solution.py:116
  168.5 8.7 copy.94
  177.2 74.9 %while.28 = (s32[]{:T(128)}, bf16[2,2,256,12,64]{2,4,3,1,0:T(8,128)(2,1)}, f32[2,2,12,256]{3,2,1,0:T(8,128)S(1)}, bf16[2,2,1024,768]{2,3,1,0:T(8,128)(2,1)}, bf1...) while((s32[]{:T(128)}, bf16[2,2,256,12,64]{2,4,3,1,0:T(8,128)(2,1)}, ...), condition=%wide.region_5.6_spmd.clone, body=%wide.region_2.5_spmd.sunk.clone | while | flops 1667229696 | bytes 96952408 | solution.py:140
  177.2 3.7 constant_dynamic-slice_fusion.10
  180.9 10.2 multiply_reduce_fusion.11
  191.1 11.7 %fusion.143 = f32[2,12,256]{2,1,0:T(8,128)S(1)} fusion(f32[2,12,256,1024]{3,2,1,0:T(8,128)} %get-tuple-element.385, f32[2,12,256]{2,1,0:T(8,128)S(1)} %get-tuple-element.386), kind=kLoop, calls=%fused_computation.3.clone.1.clone | loop fusion | flops 18868224 | bytes 25214976 | tf_op jit(solution)/shard_map/while/body/eval_jaxpr/reduce_sum | solution.py:135
  202.8 11.8 %bitcast_dynamic-update-slice_fusion.9 = bf16[2,2,256,12,64]{2,4,3,1,0:T(8,128)(2,1)} fusion(bf16[2,2,256,12,64]{2,4,3,1,0:T(8,128)(2,1)} %get-tuple-element.425, s32[]{:T(128)S(6)} %copy.125, bf16[2,1024,12,64]{1,3,2,0:T(8,128)(2,1)S(1)} %bitcast.191, f32[2,12,256,1024]{3,2,1,0:T(8,128)} %get-tuple-element.385, ...), kind=kOutput, calls=%fused_computation.5.clone.1.clone | convolution fusion | flops 830472192 | bytes 29933572 | tf_op jit(solution)/shard_map/while/body/eval_jaxpr/ghqk,gkhd->gqhd/dot_general | solution.py:137
  214.6 3.6 constant_dynamic-slice_fusion.10
  218.3 10.3 multiply_reduce_fusion.11
  228.5 11.8 %fusion.143 = f32[2,12,256]{2,1,0:T(8,128)S(1)} fusion(f32[2,12,256,1024]{3,2,1,0:T(8,128)} %get-tuple-element.385, f32[2,12,256]{2,1,0:T(8,128)S(1)} %get-tuple-element.386), kind=kLoop, calls=%fused_computation.3.clone.1.clone | loop fusion | flops 18868224 | bytes 25214976 | tf_op jit(solution)/shard_map/while/body/eval_jaxpr/reduce_sum | solution.py:135
  240.4 11.8 %bitcast_dynamic-update-slice_fusion.9 = bf16[2,2,256,12,64]{2,4,3,1,0:T(8,128)(2,1)} fusion(bf16[2,2,256,12,64]{2,4,3,1,0:T(8,128)(2,1)} %get-tuple-element.425, s32[]{:T(128)S(6)} %copy.125, bf16[2,1024,12,64]{1,3,2,0:T(8,128)(2,1)S(1)} %bitcast.191, f32[2,12,256,1024]{3,2,1,0:T(8,128)} %get-tuple-element.385, ...), kind=kOutput, calls=%fused_computation.5.clone.1.clone | convolution fusion | flops 830472192 | bytes 29933572 | tf_op jit(solution)/shard_map/while/body/eval_jaxpr/ghqk,gkhd->gqhd/dot_general | solution.py:137
  252.2 5.0 fusion.90
  259.5 11.3 fusion.40
  270.8 16.6 %fusion.93 = (bf16[3072]{0:T(1024)(128)(2,1)}, bf16[4,256,3072]{2,1,0:T(8,128)(2,1)}) fusion(f32[4,256,3072]{2,1,0:T(8,128)} %fusion.40, f32[3072]{0:T(1024)S(1)} %bitcast.210, bf16[3072,768]{1,0:T(8,128)(2,1)} %all-gather.22.cloned.1.call-done, bf16[4,256,768]{2,1,0:T(8,128)(2,1)S(1)} %copy-done.27, f32[4,768]{1,0:T(4,128)S(1)} %copy-done.36), kind=kOutput, calls=%fused_computation.174 | convolution fusion | flops 4903400448 | bytes 25196544 | tf_op jit(solution)/shard_map/scd,fd->scf/dot_general | solution.py:164
  287.4 10.2 multiply_reduce_fusion.2
  297.6 15.1 %fusion.67 = (f32[4,768]{1,0:T(4,128)}, bf16[4,256,768]{2,1,0:T(8,128)(2,1)}, f32[4,768]{1,0:T(4,128)}, f32[4,256,768]{2,1,0:T(8,128)S(1)}) fusion(bf16[4,256,768]{2,1,0:T(8,128)(2,1)S(1)} %copy-done.27, f32[768]{0:T(1024)S(1)} %copy-done.65, f32[4,256,768]{2,1,0:T(8,128)S(1)} %copy-done.18, f32[4,768]{1,0:T(4,128)S(1)} %copy-done.36, ...), kind=kOutput, calls=%fused_computation.96 | convolution fusion | flops 4877445120 | bytes 33114112 | tf_op jit(solution)/shard_map/scf,fd->scd/dot_general | solution.py:153
  317.4 178.6 %while.29 = (s32[]{:T(128)}, f32[2,2,256,12,64]{2,4,3,1,0:T(8,128)}, bf16[2,2,1024,768]{2,3,1,0:T(8,128)(2,1)}, bf16[2,2,1024,768]{2,3,1,0:T(8,128)(2,1)}, bf16[...) while((s32[]{:T(128)}, ...), condition=%wide.region_12.13_spmd.clone, body=%wide.region_10.12_spmd.sunk.clone | while | flops 4105562112 | bytes 316326176 | solution.py:223
  317.6 4.4 constant_dynamic-slice_fusion.12
  323.3 11.5 fusion.153
  334.8 12.2 %fusion.154 = bf16[2,12,64,1024]{3,2,1,0:T(8,128)(2,1)} fusion(f32[2,12,256,1024]{3,2,1,0:T(8,128)} %fusion.153, f32[2,12,256]{2,1,0:T(8,128)S(1)} %dynamic-slice_bitcast_fusion.3, bf16[2,2,256,12,64]{2,4,3,1,0:T(8,128)(2,1)S(1)} %copy-done.6, s32[]{:T(128)S(6)} %copy.135), kind=kOutput, calls=%fused_computation.18.clone.1.clone | convolution fusion | flops 824180736 | bytes 29130756 | tf_op jit(solution)/shard_map/while/body/eval_jaxpr/ghqk,gqhd->gkhd/dot_general | solution.py:200
  347.0 17.6 %multiply_reduce_fusion.12 = (f32[2,12,256]{2,1,0:T(8,128)S(1)}, f32[2,12,256,1024]{3,2,1,0:T(8,128)}) fusion(f32[2,12,256,1024]{3,2,1,0:T(8,128)} %fusion.153, f32[2,12,256]{2,1,0:T(8,128)S(1)} %dynamic-slice_bitcast_fusion.3, bf16[2,1024,12,64]{1,3,2,0:T(8,128)(2,1)} %bitcast.188, bf16[2,2,256,12,64]{2,4,3,1,0:T(8,128)(2,1)} %get-tuple-element.461, ...), kind=kOutput, calls=%fused_computation.15.clone.1.clone | convolution fusion | flops 830466048 | bytes 54312964 | tf_op jit(solution)/shard_map/while/body/eval_jaxpr/gqhd,gkhd->ghqk/dot_general | solution.py:203
  364.6 21.7 %multiply_convert_fusion.9 = bf16[2,12,256,1024]{3,2,1,0:T(8,128)(2,1)} fusion(f32[2,12,256,1024]{3,2,1,0:T(8,128)} %get-tuple-element.404, f32[2,12,256,1024]{3,2,1,0:T(8,128)} %fusion.153, f32[2,12,256]{2,1,0:T(8,128)S(1)} %get-tuple-element.405, f32[2,12,256]{2,1,0:T(8,128)S(1)} %dynamic-slice_bitcast_fusion.3), kind=kLoop, calls=%fused_computation.14.clone.1.clone | loop fusion | flops 31457280 | bytes 62963712 | tf_op jit(solution)/shard_map/while/body/eval_jaxpr/convert_element_type | solution.py:207
  386.3 8.5 bitcast_dynamic-update-slice_fusion.11
  394.8 8.3 broadcast_multiply_fusion.12
  403.1 3.5 constant_dynamic-update-slice_fusion.10
  406.6 4.4 constant_dynamic-slice_fusion.12
  412.4 11.5 fusion.153
  423.9 12.2 %fusion.154 = bf16[2,12,64,1024]{3,2,1,0:T(8,128)(2,1)} fusion(f32[2,12,256,1024]{3,2,1,0:T(8,128)} %fusion.153, f32[2,12,256]{2,1,0:T(8,128)S(1)} %dynamic-slice_bitcast_fusion.3, bf16[2,2,256,12,64]{2,4,3,1,0:T(8,128)(2,1)S(1)} %copy-done.6, s32[]{:T(128)S(6)} %copy.135), kind=kOutput, calls=%fused_computation.18.clone.1.clone | convolution fusion | flops 824180736 | bytes 29130756 | tf_op jit(solution)/shard_map/while/body/eval_jaxpr/ghqk,gqhd->gkhd/dot_general | solution.py:200
  436.1 17.6 %multiply_reduce_fusion.12 = (f32[2,12,256]{2,1,0:T(8,128)S(1)}, f32[2,12,256,1024]{3,2,1,0:T(8,128)}) fusion(f32[2,12,256,1024]{3,2,1,0:T(8,128)} %fusion.153, f32[2,12,256]{2,1,0:T(8,128)S(1)} %dynamic-slice_bitcast_fusion.3, bf16[2,1024,12,64]{1,3,2,0:T(8,128)(2,1)} %bitcast.188, bf16[2,2,256,12,64]{2,4,3,1,0:T(8,128)(2,1)} %get-tuple-element.461, ...), kind=kOutput, calls=%fused_computation.15.clone.1.clone | convolution fusion | flops 830466048 | bytes 54312964 | tf_op jit(solution)/shard_map/while/body/eval_jaxpr/gqhd,gkhd->ghqk/dot_general | solution.py:203
  453.7 21.7 %multiply_convert_fusion.9 = bf16[2,12,256,1024]{3,2,1,0:T(8,128)(2,1)} fusion(f32[2,12,256,1024]{3,2,1,0:T(8,128)} %get-tuple-element.404, f32[2,12,256,1024]{3,2,1,0:T(8,128)} %fusion.153, f32[2,12,256]{2,1,0:T(8,128)S(1)} %get-tuple-element.405, f32[2,12,256]{2,1,0:T(8,128)S(1)} %dynamic-slice_bitcast_fusion.3), kind=kLoop, calls=%fused_computation.14.clone.1.clone | loop fusion | flops 31457280 | bytes 62963712 | tf_op jit(solution)/shard_map/while/body/eval_jaxpr/convert_element_type | solution.py:207
  475.4 8.5 bitcast_dynamic-update-slice_fusion.11
  483.9 8.3 broadcast_multiply_fusion.12
  496.0 8.7 copy.102
  504.7 8.7 copy.106
  515.2 4.7 bitcast_convert_fusion.3
  520.0 12.4 %bitcast_convert_fusion = bf16[3072,768]{1,0:T(8,128)(2,1)} fusion(bf16[4,256,768]{2,1,0:T(8,128)(2,1)S(1)} %copy-done.28, f32[4,768]{1,0:T(4,128)S(1)} %copy-done.37, f32[4,256,3072]{2,1,0:T(8,128)} %fusion.40, f32[3072]{0:T(1024)S(1)} %bitcast.212), kind=kOutput, calls=%fused_computation.53 | convolution fusion | flops 4868014080 | bytes 18898944 | tf_op jit(solution)/shard_map/scf,scd->fd/dot_general | solution.py:160
  534.4 10.0 bitcast_convert_fusion.1
  548.7 14.7 %reduce-scatter.9.cloned.1.call-done = bf16[4,256,768]{2,1,0:T(8,128)(2,1)} async-done(((bf16[4,1024,768]{2,1,0:T(8,128)(2,1)}), bf16[4,256,768]{2,1,0:T(8,128)(2,1)}) %reduce-scatter.9.cloned.1.call-update) | async-done | bytes 1572880 | tf_op jit(solution)/shard_map/reduce_scatter | solution.py:234
  566.6 4.4 bitcast_multiply_fusion
  579.1 3.8 copy.105
  582.9 7.0 subtract_convert_fusion.1
  589.9 34.6 %reduce-scatter.11.cloned.1.call-done = bf16[4,256,768]{2,1,0:T(8,128)(2,1)} async-done(((bf16[4,1024,768]{2,1,0:T(8,128)(2,1)}), bf16[4,256,768]{2,1,0:T(8,128)(2,1)}) %reduce-scatter.11.cloned.1.call-update) | async-done | bytes 1572880 | tf_op jit(solution)/shard_map/reduce_scatter | solution.py:240
  624.6 9.1 fusion.64
  636.0 4.9 convolution_convert_fusion
  641.1 7.9 bitcast_convert_fusion.2
  653.3 50.5 %reduce-scatter.19.cloned.1.call-done = bf16[768,768]{1,0:T(8,128)(2,1)} async-done(((bf16[3072,768]{1,0:T(8,128)(2,1)}), bf16[768,768]{1,0:T(8,128)(2,1)}) %reduce-scatter.19.cloned.1.call-update) | async-done | bytes 1179664 | tf_op jit(solution)/shard_map/reduce_scatter | solution.py:300
  703.8 50.3 %reduce-scatter.17.cloned.1.call-done = bf16[192,3072]{1,0:T(8,128)(2,1)} async-done(((bf16[768,3072]{1,0:T(8,128)(2,1)}), bf16[192,3072]{1,0:T(8,128)(2,1)}) %reduce-scatter.17.cloned.1.call-update) | async-done | bytes 1179664 | tf_op jit(solution)/shard_map/reduce_scatter | solution.py:294
  754.2 10.3 all-reduce.9
  764.8 4.5 fusion.63
  769.3 8.0 reduce-scatter.23.cloned.1.call-done
  777.4 28.7 %reduce-scatter.21.cloned.1.call-done = bf16[1152,128]{1,0:T(8,128)(2,1)} async-done(((bf16[4608,128]{1,0:T(8,128)(2,1)}), bf16[1152,128]{1,0:T(8,128)(2,1)}) %reduce-scatter.21.cloned.1.call-update) | async-done | bytes 294928 | tf_op jit(solution)/shard_map/reduce_scatter | solution.py:306
  806.1 43.0 %reduce-scatter.13.cloned.1.call-done = bf16[192,2304]{1,0:T(8,128)(2,1)} async-done(((bf16[768,2304]{1,0:T(8,128)(2,1)}), bf16[192,2304]{1,0:T(8,128)(2,1)}) %reduce-scatter.13.cloned.1.call-update) | async-done | bytes 884752 | tf_op jit(solution)/shard_map/reduce_scatter | solution.py:288
  849.1 306.4 %all-reduce.12 = (f32[192,2304]{1,0:T(8,128)}, f32[192,768]{1,0:T(8,128)}, f32[192,3072]{1,0:T(8,128)}, f32[768]{0:T(1024)}, f32[768,768]{1,0:T(8,128)}, /*index...) all-reduce(bf16[192,2304]{1,0:T(8,128)(2,1)} %reduce-scatter.13.clo, ...), channel_id=1, replica_groups=mesh['dp'=8,'seq'=4] {'dp'}, use_global_device_ids=true, to_apply=%region_18.19 | all-reduce | flops 1952192 | bytes 11718144 | tf_op jit(solution)/shard_map/psum | solution.py:322
  (276 shorter events, 73.5 us)
Async XLA Ops:
  7.2 22.9 %copy-start = (bf16[1024,128]{1,0:T(8,128)(2,1)S(1)}, bf16[1024,128]{1,0:T(8,128)(2,1)}, u32[]{:S(2)}) copy-start(bf16[1024,128]{1,0:T(8,128)(2,1)} %param.20) | copy-start | bytes 786436
  7.2 22.2 %copy-start.10 = (bf16[4,256,768]{2,1,0:T(8,128)(2,1)S(1)}, bf16[4,256,768]{2,1,0:T(8,128)(2,1)}, u32[]{:S(2)}) copy-start(bf16[4,256,768]{2,1,0:T(8,128)(2,1)} %param.19) | copy-start | bytes 4718596
  7.2 22.9 %copy-start.71 = (s32[4]{0:T(128)S(1)}, s32[4]{0:T(128)}, u32[]{:S(2)}) copy-start(s32[4]{0:T(128)} %param.21) | copy-start | bytes 52
  7.2 23.1 %all-gather.10.cloned.1.call-start = ((), (), s32[]{:S(2)}) async-start(), calls=%async_computation.8 | async-start | bytes 1474560 | tf_op jit(solution)/shard_map/all_gather | solution.py:78
  8.0 54.3 %all-gather.12.cloned.1.call-start = ((), (), s32[]{:S(2)}) async-start(), calls=%async_computation.9 | async-start | bytes 4423680 | tf_op jit(solution)/shard_map/all_gather | solution.py:72
  8.7 113.2 %all-gather.14.cloned.1.call-start = ((), (), s32[]{:S(2)}) async-start(), calls=%async_computation.10 | async-start | bytes 7864320 | tf_op jit(solution)/shard_map/all_gather | solution.py:117
  21.7 46.7 %copy-start.42 = (f32[768]{0:T(1024)}, f32[768]{0:T(1024)S(1)}, u32[]{:S(2)}) copy-start(f32[768]{0:T(1024)S(1)} %convert_element_type.165) | copy-start | bytes 9220
  29.4 39.0 %copy-start.40 = (f32[4,256]{1,0:T(4,128)}, f32[4,256]{1,0:T(4,128)S(1)}, u32[]{:S(2)}) copy-start(f32[4,256]{1,0:T(4,128)S(1)} %broadcast_multiply_fusion.9) | copy-start | bytes 12292
  30.1 38.4 %copy-start.44 = (f32[4,256]{1,0:T(4,128)}, f32[4,256]{1,0:T(4,128)S(1)}, u32[]{:S(2)}) copy-start(f32[4,256]{1,0:T(4,128)S(1)} %add_rsqrt_fusion.1) | copy-start | bytes 12292
  33.2 35.3 %copy-start.34 = (f32[4,768]{1,0:T(4,128)}, f32[4,768]{1,0:T(4,128)S(1)}, u32[]{:S(2)}) copy-start(f32[4,768]{1,0:T(4,128)S(1)} %get-tuple-element.257) | copy-start | bytes 36868
  33.2 35.3 %copy-start.48 = (f32[4,768]{1,0:T(4,128)}, f32[4,768]{1,0:T(4,128)S(1)}, u32[]{:S(2)}) copy-start(f32[4,768]{1,0:T(4,128)S(1)} %get-tuple-element.256) | copy-start | bytes 36868
  73.5 95.0 %all-gather.16.cloned.1.call-start = ((), (), s32[]{:S(2)}) async-start(), calls=%async_computation.11 | async-start | bytes 7864320 | tf_op jit(solution)/shard_map/all_gather | solution.py:116
  74.6 15.8 %copy-start.24 = (f32[4,256,64]{1,2,0:T(8,128)}, f32[4,256,64]{1,2,0:T(8,128)S(1)}, u32[]{:S(2)}) copy-start(f32[4,256,64]{1,2,0:T(8,128)S(1)} %get-tuple-element.250) | copy-start | bytes 786436
  79.2 16.8 %copy-start.8 = (f32[4,256,768]{2,1,0:T(8,128)}, f32[4,256,768]{2,1,0:T(8,128)S(1)}, u32[]{:S(2)}) copy-start(f32[4,256,768]{2,1,0:T(8,128)S(1)} %copy.90) | copy-start | bytes 9437188
  102.7 149.5 %all-gather.18.cloned.1.call-start = ((), (), s32[]{:S(2)}) async-start(), calls=%async_computation.12 | async-start | bytes 1474560 | tf_op jit(solution)/shard_map/all_gather | solution.py:73
  103.3 156.1 %all-gather.20.cloned.1.call-start = ((), (), s32[]{:S(2)}) async-start(), calls=%async_computation.13 | async-start | bytes 5898240 | tf_op jit(solution)/shard_map/all_gather | solution.py:74
  103.8 166.9 %all-gather.22.cloned.1.call-start = ((), (), s32[]{:S(2)}) async-start(), calls=%async_computation.14 | async-start | bytes 5898240 | tf_op jit(solution)/shard_map/all_gather | solution.py:76
  104.6 458.9 %reduce-scatter.9.cloned.1.call-start = ((), (), s32[]{:S(2)}) async-start(), calls=%async_computation.15 | async-start | bytes 7864320 | tf_op jit(solution)/shard_map/reduce_scatter | solution.py:234
  177.2 75.0 %copy-start.11 = (bf16[4,256,768]{2,1,0:T(8,128)(2,1)S(1)}, bf16[4,256,768]{2,1,0:T(8,128)(2,1)}, u32[]{:S(2)}) copy-start(bf16[4,256,768]{2,1,0:T(8,128)(2,1)} %param.19) | copy-start | bytes 4718596
  177.2 75.0 %copy-start.38 = (f32[4,768]{1,0:T(4,128)S(1)}, f32[4,768]{1,0:T(4,128)}, u32[]{:S(2)}) copy-start(f32[4,768]{1,0:T(4,128)} %get-tuple-element.258) | copy-start | bytes 36868
  257.3 40.3 %copy-start.46 = (f32[4,256]{1,0:T(4,128)}, f32[4,256]{1,0:T(4,128)S(1)}, u32[]{:S(2)}) copy-start(f32[4,256]{1,0:T(4,128)S(1)} %broadcast_multiply_fusion.8) | copy-start | bytes 12292
  259.4 38.2 %copy-start.67 = (f32[4,256]{1,0:T(4,128)}, f32[4,256]{1,0:T(4,128)S(1)}, u32[]{:S(2)}) copy-start(f32[4,256]{1,0:T(4,128)S(1)} %add_rsqrt_fusion) | copy-start | bytes 12292
  259.4 11.3 copy-start.27
  259.4 11.3 copy-start.36
  259.5 11.3 copy-start.54
  270.8 16.6 %copy-start.18 = (f32[4,256,768]{2,1,0:T(8,128)S(1)}, f32[4,256,768]{2,1,0:T(8,128)}, u32[]{:S(2)}) copy-start(f32[4,256,768]{2,1,0:T(8,128)} %copy-done.17) | copy-start | bytes 9437188
  270.8 16.6 %copy-start.73 = (bf16[768,3072]{1,0:T(8,128)(2,1)S(1)}, bf16[768,3072]{1,0:T(8,128)(2,1)}, u32[]{:S(2)}) copy-start(bf16[768,3072]{1,0:T(8,128)(2,1)} %all-gather.20.cloned.1.call-done) | copy-start | bytes 14155780
  287.4 10.2 copy-start.23
  287.4 10.2 copy-start.65
  297.6 16.7 %copy-start.31 = (bf16[768,768]{1,0:T(8,128)(2,1)S(1)}, bf16[768,768]{1,0:T(8,128)(2,1)}, u32[]{:S(2)}) copy-start(bf16[768,768]{1,0:T(8,128)(2,1)} %all-gather.18.cloned.1.call-done) | copy-start | bytes 3538948
  323.3 11.5 copy-start.6
  364.6 21.7 %copy-start.14 = (f32[2,2,256,12,64]{2,4,3,1,0:T(8,128)S(1)}, f32[2,2,256,12,64]{2,4,3,1,0:T(8,128)}, u32[]{:S(2)}) copy-start(f32[2,2,256,12,64]{2,4,3,1,0:T(8,128)} %get-tuple-element.446) | copy-start | bytes 9437188 | tf_op jit(solution)/shard_map/while
  394.8 8.3 copy-start.15
  394.8 8.3 copy-start.2
  412.4 11.5 copy-start.6
  453.7 21.7 %copy-start.14 = (f32[2,2,256,12,64]{2,4,3,1,0:T(8,128)S(1)}, f32[2,2,256,12,64]{2,4,3,1,0:T(8,128)}, u32[]{:S(2)}) copy-start(f32[2,2,256,12,64]{2,4,3,1,0:T(8,128)} %get-tuple-element.446) | copy-start | bytes 9437188 | tf_op jit(solution)/shard_map/while
  483.9 8.3 copy-start.15
  483.9 8.3 copy-start.2
  504.6 119.9 %reduce-scatter.11.cloned.1.call-start = ((), (), s32[]{:S(2)}) async-start(), calls=%async_computation.16 | async-start | bytes 7864320 | tf_op jit(solution)/shard_map/reduce_scatter | solution.py:240
  513.4 139.9 %reduce-scatter.15.cloned.1.call-start = ((), (), s32[]{:S(2)}) async-start(), calls=%async_computation.18 | async-start | bytes 1474560 | tf_op jit(solution)/shard_map/reduce_scatter | solution.py:291
  519.9 183.9 %reduce-scatter.19.cloned.1.call-start = ((), (), s32[]{:S(2)}) async-start(), calls=%async_computation.20 | async-start | bytes 5898240 | tf_op jit(solution)/shard_map/reduce_scatter | solution.py:300
  532.5 221.6 %reduce-scatter.17.cloned.1.call-start = ((), (), s32[]{:S(2)}) async-start(), calls=%async_computation.19 | async-start | bytes 5898240 | tf_op jit(solution)/shard_map/reduce_scatter | solution.py:294
  544.4 233.0 %reduce-scatter.23.cloned.1.call-start = ((), (), s32[]{:S(2)}) async-start(), calls=%async_computation.22 | async-start | bytes 327680 | tf_op jit(solution)/shard_map/reduce_scatter | solution.py:318
  548.7 17.8 %copy-start.25 = (f32[4,256,64]{1,2,0:T(8,128)S(1)}, f32[4,256,64]{1,2,0:T(8,128)}, u32[]{:S(2)}) copy-start(f32[4,256,64]{1,2,0:T(8,128)} %copy-done.24) | copy-start | bytes 786436
  582.9 41.6 %copy-start.35 = (f32[4,768]{1,0:T(4,128)S(1)}, f32[4,768]{1,0:T(4,128)}, u32[]{:S(2)}) copy-start(f32[4,768]{1,0:T(4,128)} %copy-done.34) | copy-start | bytes 36868
  582.9 41.6 %copy-start.41 = (f32[4,256]{1,0:T(4,128)S(1)}, f32[4,256]{1,0:T(4,128)}, u32[]{:S(2)}) copy-start(f32[4,256]{1,0:T(4,128)} %copy-done.40) | copy-start | bytes 12292
  582.9 41.6 %copy-start.43 = (f32[768]{0:T(1024)S(1)}, f32[768]{0:T(1024)}, u32[]{:S(2)}) copy-start(f32[768]{0:T(1024)} %copy-done.42) | copy-start | bytes 9220
  582.9 41.6 %copy-start.45 = (f32[4,256]{1,0:T(4,128)S(1)}, f32[4,256]{1,0:T(4,128)}, u32[]{:S(2)}) copy-start(f32[4,256]{1,0:T(4,128)} %copy-done.44) | copy-start | bytes 12292
  624.5 9.3 copy-start.59
  624.5 9.3 copy-start.57
  624.6 9.3 copy-start.56
  624.6 9.3 copy-start.58
  624.6 9.3 copy-start.21
  624.6 9.9 copy-start.72
  624.6 11.4 copy-start.61
  633.7 7.4 copy-start.12
  633.8 7.4 copy-start.26
  635.9 170.2 %reduce-scatter.21.cloned.1.call-start = ((), (), s32[]{:S(2)}) async-start(), calls=%async_computation.21 | async-start | bytes 1474560 | tf_op jit(solution)/shard_map/reduce_scatter | solution.py:306
  640.8 208.3 %reduce-scatter.13.cloned.1.call-start = ((), (), s32[]{:S(2)}) async-start(), calls=%async_computation.17 | async-start | bytes 4423680 | tf_op jit(solution)/shard_map/reduce_scatter | solution.py:288
  649.0 105.1 %copy-start.62 = (bf16[3072]{0:T(1024)(128)(2,1)S(1)}, bf16[3072]{0:T(1024)(128)(2,1)}, u32[]{:S(2)}) copy-start(bf16[3072]{0:T(1024)(128)(2,1)} %get-tuple-element.264) | copy-start | bytes 18436
  649.0 105.1 %copy-start.70 = (bf16[768]{0:T(1024)(128)(2,1)S(1)}, bf16[768]{0:T(1024)(128)(2,1)}, u32[]{:S(2)}) copy-start(bf16[768]{0:T(1024)(128)(2,1)} %get-tuple-element.160) | copy-start | bytes 4612
  764.8 84.3 %copy-start.30 = (bf16[768,768]{1,0:T(8,128)(2,1)S(1)}, bf16[768,768]{1,0:T(8,128)(2,1)}, u32[]{:S(2)}) copy-start(bf16[768,768]{1,0:T(8,128)(2,1)} %reduce-scatter.19.cloned.1.call-done) | copy-start | bytes 3538948
  764.8 84.3 %copy-start.33 = (bf16[192,768]{1,0:T(8,128)(2,1)S(1)}, bf16[192,768]{1,0:T(8,128)(2,1)}, u32[]{:S(2)}) copy-start(bf16[192,768]{1,0:T(8,128)(2,1)} %reduce-scatter.15.cloned.1.call-done) | copy-start | bytes 884740
  764.8 390.7 %copy-start.1 = (bf16[1024,128]{1,0:T(8,128)(2,1)S(1)}, bf16[1024,128]{1,0:T(8,128)(2,1)}, u32[]{:S(2)}) copy-start(bf16[1024,128]{1,0:T(8,128)(2,1)} %param.20) | copy-start | bytes 786436
  (32 other events, 98.4 us)
Sparse Core Ops, SparseCore 0:
  9.6 20.2 all-gather.9
  31.5 30.7 all-gather.11
  73.6 46.4 all-gather.13
  122.1 46.3 all-gather.15
  169.9 17.4 all-gather.17
  188.8 37.4 all-gather.19
  227.9 37.4 all-gather.21
  504.8 58.6 reduce-scatter.8
  566.1 58.3 reduce-scatter.10
  627.5 25.7 reduce-scatter.14
  656.0 47.8 reduce-scatter.18
  706.2 47.8 reduce-scatter.16
  757.3 20.0 reduce-scatter.22
  780.3 25.7 reduce-scatter.20
  808.7 40.4 reduce-scatter.12
where the time goes:
time: 1170 us; the launch traced here: 1160 us
  blocking collectives  336 us (29%)
  waiting for transfers between devices  302 us (26%)
  matrix products  279 us (24%)
  local copies, waits for them, and re-layouts  113 us (10%)
  other arithmetic  113 us (10%)
  between operations  17.8 us (2%)
    psum x1, blocking collectives, shards(): lax.psum((shares[0], shares[1], shares[2], shares[3], shares[4], shares[5...  306 us
    reduce_scatter x1, waiting for transfers between devices, shards(): lax.psum_scatter(terms[4].astype(jnp.bfloat16), 'seq', scatter_dimension=...  50.5 us
    reduce_scatter x1, waiting for transfers between devices, shards(): lax.psum_scatter(terms[2].astype(jnp.bfloat16), 'seq', scatter_dimension=...  50.3 us
    convert_element_type x2, other arithmetic, attend_back(): scores_grad = (probs * (probs_grad - center)).astype(low_type)  43.4 us
    reduce_scatter x1, waiting for transfers between devices, shards(): lax.psum_scatter(terms[0].astype(jnp.bfloat16), 'seq', scatter_dimension=...  43 us
    all_gather x1, waiting for transfers between devices, shards(): lax.all_gather(keys_local, 'seq', axis=1, tiled=True)  37.9 us
    dot_general x2, matrix products, attend_back(): jnp.einsum('gqhd,gkhd->ghqk', mixed_grad_b, values_h, preferred_element_t...  35.2 us
    reduce_scatter x1, waiting for transfers between devices, shards(): lax.psum_scatter(values_term.reshape(seqs, length, width).astype(jnp.bflo...  34.6 us
  transfers between devices with their start and end apart: 15, of which 10 were waited for; matrix products, arithmetic and copies ran while one was open for 22% of the time, Pallas kernels for 0%

commit v1 on v0

--- a/solution.py
+++ b/solution.py
@@ -7,6 +7,19 @@
 
 HEADS = 12
 EPSILON = 1e-05
+
+
+def ring_gather(x, axis, dim):
+    ways = lax.axis_size(axis)
+    up = [(d, (d + 1) % ways) for d in range(ways)]
+    down = [(d, (d - 1) % ways) for d in range(ways)]
+    earlier, later = ([x], [x])
+    for _ in range(ways // 2):
+        earlier.append(lax.ppermute(earlier[-1], axis, up))
+    for _ in range((ways - 1) // 2):
+        later.append(lax.ppermute(later[-1], axis, down))
+    line = jnp.concatenate([*earlier[::-1], *later[1:]], axis=dim)
+    return jnp.roll(line, (lax.axis_index(axis) - ways // 2) * x.shape[dim], axis=dim)
 
 
 def rotate_half(values):
@@ -113,7 +126,7 @@
     )
     values_local = value_raw.astype(low_type)
     keys_all, values_all = (
-        lax.all_gather(keys_local, "seq", axis=1, tiled=True),
+        ring_gather(keys_local, "seq", 1),
         lax.all_gather(values_local, "seq", axis=1, tiled=True),
     )
     group = grouping(seqs, span)

time: 1170 us -> 1250 us (1.068)
  local copies, waits for them, and re-layouts: 113 us -> 140 us
  blocking collectives: 336 us -> 356 us
  waiting for transfers between devices: 302 us -> 321 us
    ppermute x0 -> x3, waiting for transfers between devices: none -> 55.5 us  [the longest x2 30.6 us: ring_gather(): earlier.append(lax.ppermute(earlier[-1], axis, up))]
    all_gather x1, waiting for transfers between devices: 37.9 us -> 0.01 us  [shards(): lax.all_gather(keys_local, 'seq', axis=1, tiled=True)]
    dynamic_slice x6 -> x12, local copies, waits for them, and re-layouts: 16.7 us -> 39.9 us  [shards(): lax.map(attend, (split_groups(query), split_groups(keys_all), split_group...]
    all_gather x1, blocking collectives: 5.65 us -> 26 us  [shards(): lax.all_gather(lift_bias, 'seq', axis=0, tiled=True)]
  transfers between devices with their start and end apart: 15 -> 18, of which waited for: 10 -> 11; matrix products, arithmetic and copies ran while one was open for 22% -> 26% of each run, Pallas kernels for 0% -> 0%
where the time goes in v1:
time: 1250 us; the launch traced here: 1240 us
  blocking collectives  356 us (28%)
  waiting for transfers between devices  321 us (26%)
  matrix products  288 us (23%)
  local copies, waits for them, and re-layouts  140 us (11%)
  other arithmetic  113 us (9%)
  between operations  18 us (1%)
    psum x1, blocking collectives, shards(): lax.psum((shares[0], shares[1], shares[2], shares[3], shares[4], shares[5...  306 us
    reduce_scatter x1, waiting for transfers between devices, shards(): lax.psum_scatter(terms[4].astype(jnp.bfloat16), 'seq', scatter_dimension=...  50.6 us
    reduce_scatter x1, waiting for transfers between devices, shards(): lax.psum_scatter(terms[2].astype(jnp.bfloat16), 'seq', scatter_dimension=...  50.3 us
    convert_element_type x2, other arithmetic, attend_back(): scores_grad = (probs * (probs_grad - center)).astype(low_type)  43.4 us
    reduce_scatter x1, waiting for transfers between devices, shards(): lax.psum_scatter(terms[0].astype(jnp.bfloat16), 'seq', scatter_dimension=...  43 us
    dynamic_slice x12, local copies, waits for them, and re-layouts, shards(): lax.map(attend, (split_groups(query), split_groups(keys_all), split_group...  39.9 us
    dot_general x2, matrix products, attend_back(): jnp.einsum('gqhd,gkhd->ghqk', mixed_grad_b, values_h, preferred_element_t...  35.1 us
    reduce_scatter x1, waiting for transfers between devices, shards(): lax.psum_scatter(values_term.reshape(seqs, length, width).astype(jnp.bflo...  34.6 us
  transfers between devices with their start and end apart: 18, of which 11 were waited for; matrix products, arithmetic and copies ran while one was open for 26% of the time, Pallas kernels for 0%

profile of v1, /device:TPU:0, one launch (start us, length us, event | category | flops | bytes accessed | tf_op | source)
XLA Modules:
  0.0 1238.9 jit_solution(10977989951317901413)
XLA Ops:
  13.3 8.5 all-reduce.10
  22.4 5.2 all-gather
  33.2 29.1 %all-gather.12.cloned.1.call-done = bf16[768,2304]{1,0:T(8,128)(2,1)} async-done(((bf16[192,2304]{1,0:T(8,128)(2,1)}), bf16[768,2304]{1,0:T(8,128)(2,1)}) %all-gather.12.cloned.1.call-update) | async-done | bytes 3538960 | tf_op jit(solution)/shard_map/all_gather | solution.py:85
  62.3 6.2 fusion.52
  68.5 3.6 copy-done.13
  81.2 5.6 split.42
  86.8 3.6 copy.90
  98.0 6.6 add_convert_fusion.2
  104.7 30.6 %collective-permute-done = bf16[4,256,768]{2,1,0:T(8,128)(2,1)} collective-permute-done((bf16[4,256,768]{2,1,0:T(8,128)(2,1)}, bf16[4,256,768]{2,1,0:T(8,128)(2,1)}, u32[]{:S(2)}, u32[]{:S(2)}) %collective-permute-start) | collective-permute-done | bytes 1572896 | tf_op jit(solution)/shard_map/ppermute | solution.py:18
  136.6 26.0 %all-gather.1 = bf16[4,1,768]{2,1,0:T(2,128)(2,1)S(1)} all-gather(bf16[1,1,768]{2,1,0:T(2,128)(2,1)S(1)} %reshape.233), channel_id=1, replica_groups=mesh['dp'=8,'seq'=4] {'seq'}, dimensions={0}, use_global_device_ids=true | all-gather | bytes 7680 | tf_op jit(solution)/shard_map/all_gather | solution.py:88
  175.3 24.8 %collective-permute-done.2 = bf16[4,256,768]{2,1,0:T(8,128)(2,1)} collective-permute-done((bf16[4,256,768]{2,1,0:T(8,128)(2,1)}, bf16[4,256,768]{2,1,0:T(8,128)(2,1)}, u32[]{:S(2)}, u32[]{:S(2)}) %collective-permute-start.2) | collective-permute-done | bytes 1572896 | tf_op jit(solution)/shard_map/ppermute | solution.py:20
  209.7 8.6 copy.92
  218.3 90.9 %while.28 = (s32[]{:T(128)}, bf16[2,2,256,12,64]{2,4,3,1,0:T(8,128)(2,1)}, f32[2,2,12,256]{3,2,1,0:T(8,128)S(1)}, bf16[2,2,1024,768]{2,3,1,0:T(8,128)(2,1)}, bf1...) while((s32[]{:T(128)}, bf16[2,2,256,12,64]{2,4,3,1,0:T(8,128)(2,1)}, ...), condition=%wide.region_5.6_spmd.clone, body=%wide.region_2.5_spmd.sunk.clone | while | flops 1667229696 | bytes 134717632 | solution.py:153
  218.3 3.8 constant_dynamic-slice_fusion.14
  225.3 3.9 constant_dynamic-slice_fusion.13
  229.2 10.2 multiply_reduce_fusion.11
  239.4 13.0 %fusion.143 = f32[2,12,256]{2,1,0:T(8,128)S(1)} fusion(f32[2,12,256,1024]{3,2,1,0:T(8,128)} %get-tuple-element.377, f32[2,12,256]{2,1,0:T(8,128)S(1)} %get-tuple-element.378), kind=kLoop, calls=%fused_computation.3.clone.1.clone | loop fusion | flops 18868224 | bytes 25214976 | tf_op jit(solution)/shard_map/while/body/eval_jaxpr/reduce_sum | solution.py:148
  252.5 10.9 bitcast_dynamic-update-slice_fusion.9
  264.6 3.7 constant_dynamic-slice_fusion.14
  271.5 3.9 constant_dynamic-slice_fusion.13
  275.4 10.2 multiply_reduce_fusion.11
  285.6 11.6 fusion.143
  297.2 10.8 bitcast_dynamic-update-slice_fusion.9
  309.2 5.4 fusion.90
  315.5 10.8 fusion.40
  326.3 28.7 %fusion.93 = (bf16[3072]{0:T(1024)(128)(2,1)}, bf16[4,256,3072]{2,1,0:T(8,128)(2,1)}) fusion(f32[4,256,3072]{2,1,0:T(8,128)} %fusion.40, f32[3072]{0:T(1024)S(1)} %bitcast.212, bf16[3072,768]{1,0:T(8,128)(2,1)} %all-gather.20.cloned.1.call-done, bf16[4,256,768]{2,1,0:T(8,128)(2,1)} %param.33, f32[4,768]{1,0:T(4,128)S(1)} %copy-done.37), kind=kOutput, calls=%fused_computation.183 | convolution fusion | flops 4903400448 | bytes 25196544 | tf_op jit(solution)/shard_map/scd,fd->scf/dot_general | solution.py:177
  355.0 10.2 multiply_reduce_fusion.2
  365.3 13.8 %fusion.67 = (f32[4,768]{1,0:T(4,128)}, bf16[4,256,768]{2,1,0:T(8,128)(2,1)}, f32[4,768]{1,0:T(4,128)}, f32[4,256,768]{2,1,0:T(8,128)S(1)}) fusion(bf16[4,256,768]{2,1,0:T(8,128)(2,1)S(1)} %copy-done.28, f32[768]{0:T(1024)S(1)} %copy-done.66, f32[4,256,768]{2,1,0:T(8,128)S(1)} %get-tuple-element.222, f32[4,768]{1,0:T(4,128)S(1)} %copy-done.37, ...), kind=kOutput, calls=%fused_computation.96 | convolution fusion | flops 4877445120 | bytes 33114112 | tf_op jit(solution)/shard_map/scf,fd->scd/dot_general | solution.py:166
  383.8 186.1 %while.29 = (s32[]{:T(128)}, f32[2,2,256,12,64]{2,4,3,1,0:T(8,128)}, bf16[2,2,1024,768]{2,3,1,0:T(8,128)(2,1)}, bf16[2,2,1024,768]{2,3,1,0:T(8,128)(2,1)}, bf16[...) while((s32[]{:T(128)}, ...), condition=%wide.region_12.13_spmd.clone, body=%wide.region_10.12_spmd.sunk.clone | while | flops 4105562112 | bytes 316326144 | solution.py:236
  384.2 4.0 constant_dynamic-slice_fusion.16
  393.9 11.5 fusion.153
  405.4 12.2 fusion.154
  417.6 17.6 %multiply_reduce_fusion.12 = (f32[2,12,256]{2,1,0:T(8,128)S(1)}, f32[2,12,256,1024]{3,2,1,0:T(8,128)}) fusion(f32[2,12,256,1024]{3,2,1,0:T(8,128)} %fusion.153, f32[2,12,256]{2,1,0:T(8,128)S(1)} %dynamic-slice_bitcast_fusion.3, bf16[2,1024,12,64]{1,3,2,0:T(8,128)(2,1)} %bitcast.189, bf16[2,2,256,12,64]{2,4,3,1,0:T(8,128)(2,1)} %get-tuple-element.453, ...), kind=kOutput, calls=%fused_computation.15.clone.1.clone | convolution fusion | flops 830466048 | bytes 54312964 | tf_op jit(solution)/shard_map/while/body/eval_jaxpr/gqhd,gkhd->ghqk/dot_general | solution.py:216
  435.1 21.7 %multiply_convert_fusion.9 = bf16[2,12,256,1024]{3,2,1,0:T(8,128)(2,1)} fusion(f32[2,12,256,1024]{3,2,1,0:T(8,128)} %get-tuple-element.396, f32[2,12,256,1024]{3,2,1,0:T(8,128)} %fusion.153, f32[2,12,256]{2,1,0:T(8,128)S(1)} %get-tuple-element.397, f32[2,12,256]{2,1,0:T(8,128)S(1)} %dynamic-slice_bitcast_fusion.3), kind=kLoop, calls=%fused_computation.14.clone.1.clone | loop fusion | flops 31457280 | bytes 62963712 | tf_op jit(solution)/shard_map/while/body/eval_jaxpr/convert_element_type | solution.py:220
  456.8 8.6 bitcast_dynamic-update-slice_fusion.11
  465.5 8.1 broadcast_multiply_fusion.12
  477.0 4.0 constant_dynamic-slice_fusion.16
  486.8 11.5 fusion.153
  498.3 12.2 fusion.154
  510.4 17.6 %multiply_reduce_fusion.12 = (f32[2,12,256]{2,1,0:T(8,128)S(1)}, f32[2,12,256,1024]{3,2,1,0:T(8,128)}) fusion(f32[2,12,256,1024]{3,2,1,0:T(8,128)} %fusion.153, f32[2,12,256]{2,1,0:T(8,128)S(1)} %dynamic-slice_bitcast_fusion.3, bf16[2,1024,12,64]{1,3,2,0:T(8,128)(2,1)} %bitcast.189, bf16[2,2,256,12,64]{2,4,3,1,0:T(8,128)(2,1)} %get-tuple-element.453, ...), kind=kOutput, calls=%fused_computation.15.clone.1.clone | convolution fusion | flops 830466048 | bytes 54312964 | tf_op jit(solution)/shard_map/while/body/eval_jaxpr/gqhd,gkhd->ghqk/dot_general | solution.py:216
  528.0 21.7 %multiply_convert_fusion.9 = bf16[2,12,256,1024]{3,2,1,0:T(8,128)(2,1)} fusion(f32[2,12,256,1024]{3,2,1,0:T(8,128)} %get-tuple-element.396, f32[2,12,256,1024]{3,2,1,0:T(8,128)} %fusion.153, f32[2,12,256]{2,1,0:T(8,128)S(1)} %get-tuple-element.397, f32[2,12,256]{2,1,0:T(8,128)S(1)} %dynamic-slice_bitcast_fusion.3), kind=kLoop, calls=%fused_computation.14.clone.1.clone | loop fusion | flops 31457280 | bytes 62963712 | tf_op jit(solution)/shard_map/while/body/eval_jaxpr/convert_element_type | solution.py:220
  549.7 8.6 bitcast_dynamic-update-slice_fusion.11
  558.4 8.1 broadcast_multiply_fusion.12
  569.9 8.7 copy.101
  578.7 8.7 copy.105
  588.8 5.1 bitcast_convert_fusion.3
  594.0 12.7 %bitcast_convert_fusion = bf16[3072,768]{1,0:T(8,128)(2,1)} fusion(bf16[4,256,768]{2,1,0:T(8,128)(2,1)S(1)} %copy-done.29, f32[4,768]{1,0:T(4,128)S(1)} %copy-done.38, f32[4,256,3072]{2,1,0:T(8,128)} %fusion.40, f32[3072]{0:T(1024)S(1)} %bitcast.214), kind=kOutput, calls=%fused_computation.53 | convolution fusion | flops 4868014080 | bytes 18898944 | tf_op jit(solution)/shard_map/scf,scd->fd/dot_general | solution.py:173
  608.6 10.0 bitcast_convert_fusion.1
  623.1 16.7 %reduce-scatter.9.cloned.1.call-done = bf16[4,256,768]{2,1,0:T(8,128)(2,1)} async-done(((bf16[4,1024,768]{2,1,0:T(8,128)(2,1)}), bf16[4,256,768]{2,1,0:T(8,128)(2,1)}) %reduce-scatter.9.cloned.1.call-update) | async-done | bytes 1572880 | tf_op jit(solution)/shard_map/reduce_scatter | solution.py:247
  642.9 4.4 bitcast_multiply_fusion
  655.4 3.8 copy.104
  659.3 7.0 subtract_convert_fusion.1
  666.2 34.6 %reduce-scatter.11.cloned.1.call-done = bf16[4,256,768]{2,1,0:T(8,128)(2,1)} async-done(((bf16[4,1024,768]{2,1,0:T(8,128)(2,1)}), bf16[4,256,768]{2,1,0:T(8,128)(2,1)}) %reduce-scatter.11.cloned.1.call-update) | async-done | bytes 1572880 | tf_op jit(solution)/shard_map/reduce_scatter | solution.py:253
  701.0 9.1 fusion.64
  712.3 4.9 convolution_convert_fusion
  717.5 7.9 bitcast_convert_fusion.2
  729.6 50.6 %reduce-scatter.19.cloned.1.call-done = bf16[768,768]{1,0:T(8,128)(2,1)} async-done(((bf16[3072,768]{1,0:T(8,128)(2,1)}), bf16[768,768]{1,0:T(8,128)(2,1)}) %reduce-scatter.19.cloned.1.call-update) | async-done | bytes 1179664 | tf_op jit(solution)/shard_map/reduce_scatter | solution.py:313
  780.2 50.3 %reduce-scatter.17.cloned.1.call-done = bf16[192,3072]{1,0:T(8,128)(2,1)} async-done(((bf16[768,3072]{1,0:T(8,128)(2,1)}), bf16[192,3072]{1,0:T(8,128)(2,1)}) %reduce-scatter.17.cloned.1.call-update) | async-done | bytes 1179664 | tf_op jit(solution)/shard_map/reduce_scatter | solution.py:307
  830.5 10.3 all-reduce.9
  841.2 4.5 fusion.63
  845.7 8.1 reduce-scatter.23.cloned.1.call-done
  853.7 28.7 %reduce-scatter.21.cloned.1.call-done = bf16[1152,128]{1,0:T(8,128)(2,1)} async-done(((bf16[4608,128]{1,0:T(8,128)(2,1)}), bf16[1152,128]{1,0:T(8,128)(2,1)}) %reduce-scatter.21.cloned.1.call-update) | async-done | bytes 294928 | tf_op jit(solution)/shard_map/reduce_scatter | solution.py:319
  882.5 43.0 %reduce-scatter.13.cloned.1.call-done = bf16[192,2304]{1,0:T(8,128)(2,1)} async-done(((bf16[768,2304]{1,0:T(8,128)(2,1)}), bf16[192,2304]{1,0:T(8,128)(2,1)}) %reduce-scatter.13.cloned.1.call-update) | async-done | bytes 884752 | tf_op jit(solution)/shard_map/reduce_scatter | solution.py:301
  925.5 306.4 %all-reduce.12 = (f32[192,2304]{1,0:T(8,128)}, f32[192,768]{1,0:T(8,128)}, f32[192,3072]{1,0:T(8,128)}, f32[768]{0:T(1024)}, f32[768,768]{1,0:T(8,128)}, /*index...) all-reduce(bf16[192,2304]{1,0:T(8,128)(2,1)} %reduce-scatter.13.clo, ...), channel_id=1, replica_groups=mesh['dp'=8,'seq'=4] {'dp'}, use_global_device_ids=true, to_apply=%region_18.19 | all-reduce | flops 1952192 | bytes 11718144 | tf_op jit(solution)/shard_map/psum | solution.py:335
  (306 shorter events, 108.0 us)
Async XLA Ops:
  7.2 22.9 %copy-start = (bf16[1024,128]{1,0:T(8,128)(2,1)S(1)}, bf16[1024,128]{1,0:T(8,128)(2,1)}, u32[]{:S(2)}) copy-start(bf16[1024,128]{1,0:T(8,128)(2,1)} %param.20) | copy-start | bytes 786436
  7.2 22.3 %copy-start.11 = (bf16[4,256,768]{2,1,0:T(8,128)(2,1)S(1)}, bf16[4,256,768]{2,1,0:T(8,128)(2,1)}, u32[]{:S(2)}) copy-start(bf16[4,256,768]{2,1,0:T(8,128)(2,1)} %param.19) | copy-start | bytes 4718596
  7.2 22.9 %copy-start.72 = (s32[4]{0:T(128)S(1)}, s32[4]{0:T(128)}, u32[]{:S(2)}) copy-start(s32[4]{0:T(128)} %param.21) | copy-start | bytes 52
  7.2 23.1 %all-gather.10.cloned.1.call-start = ((), (), s32[]{:S(2)}) async-start(), calls=%async_computation.8 | async-start | bytes 1474560 | tf_op jit(solution)/shard_map/all_gather | solution.py:91
  8.0 54.3 %all-gather.12.cloned.1.call-start = ((), (), s32[]{:S(2)}) async-start(), calls=%async_computation.9 | async-start | bytes 4423680 | tf_op jit(solution)/shard_map/all_gather | solution.py:85
  8.7 201.0 %all-gather.14.cloned.1.call-start = ((), (), s32[]{:S(2)}) async-start(), calls=%async_computation.10 | async-start | bytes 7864320 | tf_op jit(solution)/shard_map/all_gather | solution.py:130
  21.7 46.7 %copy-start.43 = (f32[768]{0:T(1024)}, f32[768]{0:T(1024)S(1)}, u32[]{:S(2)}) copy-start(f32[768]{0:T(1024)S(1)} %convert_element_type.165) | copy-start | bytes 9220
  29.5 39.0 %copy-start.41 = (f32[4,256]{1,0:T(4,128)}, f32[4,256]{1,0:T(4,128)S(1)}, u32[]{:S(2)}) copy-start(f32[4,256]{1,0:T(4,128)S(1)} %broadcast_multiply_fusion.9) | copy-start | bytes 12292
  30.1 38.4 %copy-start.45 = (f32[4,256]{1,0:T(4,128)}, f32[4,256]{1,0:T(4,128)S(1)}, u32[]{:S(2)}) copy-start(f32[4,256]{1,0:T(4,128)S(1)} %add_rsqrt_fusion.1) | copy-start | bytes 12292
  33.2 35.3 %copy-start.35 = (f32[4,768]{1,0:T(4,128)}, f32[4,768]{1,0:T(4,128)S(1)}, u32[]{:S(2)}) copy-start(f32[4,768]{1,0:T(4,128)S(1)} %get-tuple-element.255) | copy-start | bytes 36868
  33.2 35.3 %copy-start.49 = (f32[4,768]{1,0:T(4,128)}, f32[4,768]{1,0:T(4,128)S(1)}, u32[]{:S(2)}) copy-start(f32[4,768]{1,0:T(4,128)S(1)} %get-tuple-element.254) | copy-start | bytes 36868
  73.5 235.7 %all-gather.16.cloned.1.call-start = ((), (), s32[]{:S(2)}) async-start(), calls=%async_computation.11 | async-start | bytes 1474560 | tf_op jit(solution)/shard_map/all_gather | solution.py:86
  74.1 241.2 %all-gather.18.cloned.1.call-start = ((), (), s32[]{:S(2)}) async-start(), calls=%async_computation.12 | async-start | bytes 5898240 | tf_op jit(solution)/shard_map/all_gather | solution.py:87
  74.7 251.6 %all-gather.20.cloned.1.call-start = ((), (), s32[]{:S(2)}) async-start(), calls=%async_computation.13 | async-start | bytes 5898240 | tf_op jit(solution)/shard_map/all_gather | solution.py:89
  75.2 308.5 %all-gather.22.cloned.1.call-start = ((), (), s32[]{:S(2)}) async-start(), calls=%async_computation.14 | async-start | bytes 7864320 | tf_op jit(solution)/shard_map/all_gather | solution.py:199
  76.4 16.1 %copy-start.25 = (f32[4,256,64]{1,2,0:T(8,128)}, f32[4,256,64]{1,2,0:T(8,128)S(1)}, u32[]{:S(2)}) copy-start(f32[4,256,64]{1,2,0:T(8,128)S(1)} %get-tuple-element.248) | copy-start | bytes 786436
  81.2 16.8 %copy-start.8 = (f32[4,256,768]{2,1,0:T(8,128)}, f32[4,256,768]{2,1,0:T(8,128)S(1)}, u32[]{:S(2)}) copy-start(f32[4,256,768]{2,1,0:T(8,128)S(1)} %copy.89) | copy-start | bytes 9437188
  98.0 37.4 %copy-start.70 = (bf16[768]{0:T(1024)(128)(2,1)S(1)}, bf16[768]{0:T(1024)(128)(2,1)}, u32[]{:S(2)}) copy-start(bf16[768]{0:T(1024)(128)(2,1)} %param.26) | copy-start | bytes 4612
  104.6 30.7 %collective-permute-start = (bf16[4,256,768]{2,1,0:T(8,128)(2,1)}, bf16[4,256,768]{2,1,0:T(8,128)(2,1)}, u32[]{:S(2)}, u32[]{:S(2)}) collective-permute-start(bf16[4,256,768]{2,1,0:T(8,128)(2,1)} %get-tuple-element.229), channel_id=1, source_target_pairs={{0,1},{1,2},{2,3},{3,0},{4,5},{5,6},{6,7},{7,4},{8,9},{9,10},{10,1... | collective-permute-start | bytes 4718600 | tf_op jit(solution)/shard_map/ppermute | solution.py:18
  135.3 36.7 %collective-permute-start.1 = (bf16[4,256,768]{2,1,0:T(8,128)(2,1)}, bf16[4,256,768]{2,1,0:T(8,128)(2,1)}, u32[]{:S(2)}, u32[]{:S(2)}) collective-permute-start(bf16[4,256,768]{2,1,0:T(8,128)(2,1)} %collective-permute-done), channel_id=1, source_target_pairs={{0,1},{1,2},{2,3},{3,0},{4,5},{5,6},{6,7},{7,4},{8,9},{9,10},{10,1... | collective-permute-start | bytes 4718600 | tf_op jit(solution)/shard_map/ppermute | solution.py:18
  163.2 37.0 %collective-permute-start.2 = (bf16[4,256,768]{2,1,0:T(8,128)(2,1)}, bf16[4,256,768]{2,1,0:T(8,128)(2,1)}, u32[]{:S(2)}, u32[]{:S(2)}) collective-permute-start(bf16[4,256,768]{2,1,0:T(8,128)(2,1)} %get-tuple-element.229), channel_id=1, source_target_pairs={{0,3},{1,0},{2,1},{3,2},{4,7},{5,4},{6,5},{7,6},{8,11},{9,8},{10,9... | collective-permute-start | bytes 4718600 | tf_op jit(solution)/shard_map/ppermute | solution.py:20
  168.8 471.0 %reduce-scatter.9.cloned.1.call-start = ((), (), s32[]{:S(2)}) async-start(), calls=%async_computation.15 | async-start | bytes 7864320 | tf_op jit(solution)/shard_map/reduce_scatter | solution.py:247
  218.3 90.9 %copy-start.39 = (f32[4,768]{1,0:T(4,128)S(1)}, f32[4,768]{1,0:T(4,128)}, u32[]{:S(2)}) copy-start(f32[4,768]{1,0:T(4,128)} %get-tuple-element.256) | copy-start | bytes 36868
  239.4 13.0 %copy-start.5 = (bf16[1,2,1024,768]{2,3,1,0:T(8,128)(2,1)S(1)}, bf16[1,2,1024,768]{2,3,1,0:T(8,128)(2,1)}, u32[]{:S(2)}) copy-start(bf16[1,2,1024,768]{2,3,1,0:T(8,128)(2,1)} %constant_dynamic-slice_fusion.13) | copy-start | bytes 9437188 | tf_op jit(solution)/shard_map/while
  239.4 13.0 %copy-start.19 = (bf16[2,2,256,12,64]{2,4,3,1,0:T(8,128)(2,1)S(1)}, bf16[2,2,256,12,64]{2,4,3,1,0:T(8,128)(2,1)}, u32[]{:S(2)}) copy-start(bf16[2,2,256,12,64]{2,4,3,1,0:T(8,128)(2,1)} %get-tuple-element.417) | copy-start | bytes 4718596 | tf_op jit(solution)/shard_map/while
  285.6 11.6 copy-start.5
  285.6 11.6 copy-start.19
  314.7 50.6 %copy-start.17 = (f32[4,256,768]{2,1,0:T(8,128)}, f32[4,256,768]{2,1,0:T(8,128)S(1)}, u32[]{:S(2)}) copy-start(f32[4,256,768]{2,1,0:T(8,128)S(1)} %get-tuple-element.222) | copy-start | bytes 9437188
  314.7 50.5 %copy-start.47 = (f32[4,256]{1,0:T(4,128)}, f32[4,256]{1,0:T(4,128)S(1)}, u32[]{:S(2)}) copy-start(f32[4,256]{1,0:T(4,128)S(1)} %broadcast_multiply_fusion.8) | copy-start | bytes 12292
  315.2 50.0 %copy-start.68 = (f32[4,256]{1,0:T(4,128)}, f32[4,256]{1,0:T(4,128)S(1)}, u32[]{:S(2)}) copy-start(f32[4,256]{1,0:T(4,128)S(1)} %add_rsqrt_fusion) | copy-start | bytes 12292
  315.5 10.8 copy-start.37
  315.5 10.8 copy-start.55
  326.3 28.7 %copy-start.75 = (bf16[768,3072]{1,0:T(8,128)(2,1)S(1)}, bf16[768,3072]{1,0:T(8,128)(2,1)}, u32[]{:S(2)}) copy-start(bf16[768,3072]{1,0:T(8,128)(2,1)} %all-gather.18.cloned.1.call-done) | copy-start | bytes 14155780
  355.0 10.3 copy-start.24
  355.0 10.3 copy-start.28
  355.0 10.3 copy-start.66
  355.0 10.3 copy-start.74
  365.3 15.4 %copy-start.32 = (bf16[768,768]{1,0:T(8,128)(2,1)S(1)}, bf16[768,768]{1,0:T(8,128)(2,1)}, u32[]{:S(2)}) copy-start(bf16[768,768]{1,0:T(8,128)(2,1)} %all-gather.16.cloned.1.call-done) | copy-start | bytes 3538948
  393.9 11.5 copy-start.6
  435.1 21.7 %copy-start.14 = (f32[2,2,256,12,64]{2,4,3,1,0:T(8,128)S(1)}, f32[2,2,256,12,64]{2,4,3,1,0:T(8,128)}, u32[]{:S(2)}) copy-start(f32[2,2,256,12,64]{2,4,3,1,0:T(8,128)} %get-tuple-element.438) | copy-start | bytes 9437188 | tf_op jit(solution)/shard_map/while
  486.8 11.5 copy-start.6
  528.0 21.7 %copy-start.14 = (f32[2,2,256,12,64]{2,4,3,1,0:T(8,128)S(1)}, f32[2,2,256,12,64]{2,4,3,1,0:T(8,128)}, u32[]{:S(2)}) copy-start(f32[2,2,256,12,64]{2,4,3,1,0:T(8,128)} %get-tuple-element.438) | copy-start | bytes 9437188 | tf_op jit(solution)/shard_map/while
  578.6 122.3 %reduce-scatter.11.cloned.1.call-start = ((), (), s32[]{:S(2)}) async-start(), calls=%async_computation.16 | async-start | bytes 7864320 | tf_op jit(solution)/shard_map/reduce_scatter | solution.py:253
  587.4 142.2 %reduce-scatter.15.cloned.1.call-start = ((), (), s32[]{:S(2)}) async-start(), calls=%async_computation.18 | async-start | bytes 1474560 | tf_op jit(solution)/shard_map/reduce_scatter | solution.py:304
  593.9 186.2 %reduce-scatter.19.cloned.1.call-start = ((), (), s32[]{:S(2)}) async-start(), calls=%async_computation.20 | async-start | bytes 5898240 | tf_op jit(solution)/shard_map/reduce_scatter | solution.py:313
  606.7 223.7 %reduce-scatter.17.cloned.1.call-start = ((), (), s32[]{:S(2)}) async-start(), calls=%async_computation.19 | async-start | bytes 5898240 | tf_op jit(solution)/shard_map/reduce_scatter | solution.py:307
  618.6 235.1 %reduce-scatter.23.cloned.1.call-start = ((), (), s32[]{:S(2)}) async-start(), calls=%async_computation.22 | async-start | bytes 327680 | tf_op jit(solution)/shard_map/reduce_scatter | solution.py:331
  623.1 19.9 %copy-start.26 = (f32[4,256,64]{1,2,0:T(8,128)S(1)}, f32[4,256,64]{1,2,0:T(8,128)}, u32[]{:S(2)}) copy-start(f32[4,256,64]{1,2,0:T(8,128)} %copy-done.25) | copy-start | bytes 786436
  659.2 41.6 %copy-start.36 = (f32[4,768]{1,0:T(4,128)S(1)}, f32[4,768]{1,0:T(4,128)}, u32[]{:S(2)}) copy-start(f32[4,768]{1,0:T(4,128)} %copy-done.35) | copy-start | bytes 36868
  659.2 41.6 %copy-start.42 = (f32[4,256]{1,0:T(4,128)S(1)}, f32[4,256]{1,0:T(4,128)}, u32[]{:S(2)}) copy-start(f32[4,256]{1,0:T(4,128)} %copy-done.41) | copy-start | bytes 12292
  659.2 41.6 %copy-start.44 = (f32[768]{0:T(1024)S(1)}, f32[768]{0:T(1024)}, u32[]{:S(2)}) copy-start(f32[768]{0:T(1024)} %copy-done.43) | copy-start | bytes 9220
  659.3 41.6 %copy-start.46 = (f32[4,256]{1,0:T(4,128)S(1)}, f32[4,256]{1,0:T(4,128)}, u32[]{:S(2)}) copy-start(f32[4,256]{1,0:T(4,128)} %copy-done.45) | copy-start | bytes 12292
  700.9 9.3 copy-start.57
  700.9 9.3 copy-start.59
  700.9 9.3 copy-start.22
  700.9 9.9 copy-start.73
  700.9 11.4 copy-start.62
  712.2 170.2 %reduce-scatter.21.cloned.1.call-start = ((), (), s32[]{:S(2)}) async-start(), calls=%async_computation.21 | async-start | bytes 1474560 | tf_op jit(solution)/shard_map/reduce_scatter | solution.py:319
  717.2 208.3 %reduce-scatter.13.cloned.1.call-start = ((), (), s32[]{:S(2)}) async-start(), calls=%async_computation.17 | async-start | bytes 4423680 | tf_op jit(solution)/shard_map/reduce_scatter | solution.py:301
  725.4 105.1 %copy-start.63 = (bf16[3072]{0:T(1024)(128)(2,1)S(1)}, bf16[3072]{0:T(1024)(128)(2,1)}, u32[]{:S(2)}) copy-start(bf16[3072]{0:T(1024)(128)(2,1)} %get-tuple-element.262) | copy-start | bytes 18436
  725.4 105.1 %copy-start.71 = (bf16[768]{0:T(1024)(128)(2,1)S(1)}, bf16[768]{0:T(1024)(128)(2,1)}, u32[]{:S(2)}) copy-start(bf16[768]{0:T(1024)(128)(2,1)} %get-tuple-element.160) | copy-start | bytes 4612
  841.2 84.3 %copy-start.31 = (bf16[768,768]{1,0:T(8,128)(2,1)S(1)}, bf16[768,768]{1,0:T(8,128)(2,1)}, u32[]{:S(2)}) copy-start(bf16[768,768]{1,0:T(8,128)(2,1)} %reduce-scatter.19.cloned.1.call-done) | copy-start | bytes 3538948
  841.2 84.3 %copy-start.34 = (bf16[192,768]{1,0:T(8,128)(2,1)S(1)}, bf16[192,768]{1,0:T(8,128)(2,1)}, u32[]{:S(2)}) copy-start(bf16[192,768]{1,0:T(8,128)(2,1)} %reduce-scatter.15.cloned.1.call-done) | copy-start | bytes 884740
  841.2 390.7 %copy-start.1 = (bf16[1024,128]{1,0:T(8,128)(2,1)S(1)}, bf16[1024,128]{1,0:T(8,128)(2,1)}, u32[]{:S(2)}) copy-start(bf16[1024,128]{1,0:T(8,128)(2,1)} %param.20) | copy-start | bytes 786436
  (40 other events, 167.2 us)
Sparse Core Ops, SparseCore 0:
  9.6 20.2 all-gather.9
  31.5 30.7 all-gather.11
  73.6 51.7 all-gather.13
  126.9 20.2 all-gather.15
  148.6 47.6 all-gather.17
  197.7 37.4 all-gather.19
  237.3 46.3 all-gather.21
  578.7 60.9 reduce-scatter.8
  642.5 58.3 reduce-scatter.10
  703.9 25.7 reduce-scatter.14
  732.3 47.8 reduce-scatter.18
  782.6 47.8 reduce-scatter.16
  833.6 20.0 reduce-scatter.22
  856.7 25.7 reduce-scatter.20
  885.1 40.4 reduce-scatter.12
